TPU v7x, 32 devices: a whole 2x2x4 slice. The times are simulated.
32 devices in a mesh: dp: 8 (over z, y), fsdp: 4 (over x, core).
Axes of the slice: x: 2, y: 2, z: 4, core: 2. Of those that a mesh axis runs over, the one named last changes fastest.
Arguments:
- pixels: bfloat16 [8, 512, 192], P('dp', 'fsdp'), may hold values from -6 to 6
- targets: bfloat16 [8, 512, 192], P('dp', 'fsdp'), may hold values from 2 to 6
- valid_mask: int32 [8, 512, 192], P('dp', 'fsdp'), may hold values 0 or 1
- lat_weight: float32 [8, 512], P('dp', 'fsdp'), may hold values from 0.1 to 1
- segment_ids: int32 [8, 512], P('dp'), may hold values from 0 to 3, never falling along the last dimension, each value on 1 to 256 neighbouring positions
- present_vars: int32 [8, 48], P('dp'), may hold values from 0 to 1, as said below
- lead_index: int32 [8], P('dp'), may hold values from 0 to 7
- step_count: int32 [1], replicated, may hold values from 1 to 20
- w_agg: float32 [1024, 3072], P(('dp', 'fsdp')), may hold values from -0.1875 to 0.1875
- w_attn: float32 [1024, 4096], P(('dp', 'fsdp')), may hold values from -0.1875 to 0.1875
- w_mlp: float32 [1024, 8192], P(('dp', 'fsdp')), may hold values from -0.1875 to 0.1875
- w_io: float32 [1024, 944], P(('dp', 'fsdp')), may hold values from -3 to 3
- w_small: float32 [1024, 9], P(('dp', 'fsdp')), may hold values from 0.5 to 1.5
- m_agg: float32 [1024, 3072], P(('dp', 'fsdp')), may hold values from -0.00390625 to 0.00390625
- m_attn: float32 [1024, 4096], P(('dp', 'fsdp')), may hold values from -0.00390625 to 0.00390625
- m_mlp: float32 [1024, 8192], P(('dp', 'fsdp')), may hold values from -0.00390625 to 0.00390625
- m_io: float32 [1024, 944], P(('dp', 'fsdp')), may hold values from -0.00390625 to 0.00390625
- m_small: float32 [1024, 9], P(('dp', 'fsdp')), may hold values from -0.015625 to 0.015625
- v_agg: float32 [1024, 3072], P(('dp', 'fsdp')), may hold values from 2.9932032e-08 to 4.789125e-07
- v_attn: float32 [1024, 4096], P(('dp', 'fsdp')), may hold values from 2.9932032e-08 to 4.789125e-07
- v_mlp: float32 [1024, 8192], P(('dp', 'fsdp')), may hold values from 2.9932032e-08 to 4.789125e-07
- v_io: float32 [1024, 944], P(('dp', 'fsdp')), may hold values from 2.9932032e-08 to 4.789125e-07
- v_small: float32 [1024, 9], P(('dp', 'fsdp')), may hold values from 4.789125e-07 to 7.6626e-06
Outputs:
- loss: float32 [], replicated
- grad_norm: float32 [], replicated
- new_agg: float32 [1024, 3072], P(('dp', 'fsdp'))
- new_attn: float32 [1024, 4096], P(('dp', 'fsdp'))
- new_mlp: float32 [1024, 8192], P(('dp', 'fsdp'))
- new_io: float32 [1024, 944], P(('dp', 'fsdp'))
- new_small: float32 [1024, 9], P(('dp', 'fsdp'))
- copy_agg: bfloat16 [1024, 3072], P(('dp', 'fsdp'))
- copy_attn: bfloat16 [1024, 4096], P(('dp', 'fsdp'))
- copy_mlp: bfloat16 [1024, 8192], P(('dp', 'fsdp'))
- copy_io: bfloat16 [1024, 944], P(('dp', 'fsdp'))
- copy_small: bfloat16 [1024, 9], P(('dp', 'fsdp'))
- moment_agg: float32 [1024, 3072], P(('dp', 'fsdp'))
- moment_attn: float32 [1024, 4096], P(('dp', 'fsdp'))
- moment_mlp: float32 [1024, 8192], P(('dp', 'fsdp'))
- moment_io: float32 [1024, 944], P(('dp', 'fsdp'))
- moment_small: float32 [1024, 9], P(('dp', 'fsdp'))
- square_agg: float32 [1024, 3072], P(('dp', 'fsdp'))
- square_attn: float32 [1024, 4096], P(('dp', 'fsdp'))
- square_mlp: float32 [1024, 8192], P(('dp', 'fsdp'))
- square_io: float32 [1024, 944], P(('dp', 'fsdp'))
- square_small: float32 [1024, 9], P(('dp', 'fsdp'))
Inputs may be any that keep to these rules, and one draw needn't show every extreme that they name: `present_vars`: every row has at least one present variable.
All inputs are finite; a program needn't handle non-finite values. No bound on the sum of `valid_mask` on one device may be relied on, other than what follows from the above.
Results may differ from a plain program's by a relative error of at most 0.0019.
The roundings to bfloat16 on the way count: a program that leaves them out, or rounds other values in their place, can miss the bound.
Values may be sent and summed in bfloat16 or wider, within the bound.
A program may use at most 384 MiB of HBM per device.

v0:
```python
import jax
import jax.numpy as jnp
from jax import lax
from jax.sharding import PartitionSpec as P

D = 1024
HEADS = 16
HEAD_DIM = 64
FF = 4096
VARS = 48
PIX = 4
LEAD_STEPS = 8
WIDTH = VARS * PIX
SPAN = 256
MIX = WIDTH + VARS
USED = 2 * WIDTH + VARS + SPAN
norm_eps = 1e-05
clip_limit = 1.0
decay_rate = 0.05
adam_eps = 1e-08
learn_rates = (0.03, 0.03, 0.03, 0.2, 0.3)
f32 = jnp.float32
bf16 = jnp.bfloat16
highest = lax.Precision.HIGHEST


def dot(left, right, dims):
    return lax.dot_general(left, right, (dims, ((), ())), preferred_element_type=f32)


def mm(left, right):
    return dot(left, right, ((1,), (0,)))


def mm_t(left, right):
    return dot(left, right, ((1,), (1,)))


def t_mm(left, right):
    return dot(left, right, ((0,), (0,)))


def exact(eq, left, right):
    return jnp.einsum(eq, left, right, precision=highest, preferred_element_type=f32)


def norm_forward(values, gain, offset):
    average = jnp.mean(values, axis=-1, keepdims=True)
    centred = values - average
    scale = lax.rsqrt(jnp.mean(centred * centred, axis=-1, keepdims=True) + norm_eps)
    unit = centred * scale
    return ((unit * gain[None] + offset[None]).astype(bf16), unit, scale)


def norm_backward(grad, unit, scale, gain):
    inner = grad * gain[None]
    mean_inner = jnp.mean(inner, axis=-1, keepdims=True)
    mean_product = jnp.mean(inner * unit, axis=-1, keepdims=True)
    back = scale * (inner - mean_inner - unit * mean_product)
    return (back, jnp.sum(grad * unit, axis=0), jnp.sum(grad, axis=0))


def adamw(weight, grad, moment, second, step_value, learn_rate):
    moment = 0.5 * moment + 0.5 * grad
    second = 0.5 * second + 0.5 * grad * grad
    correct = 1.0 - jnp.power(f32(0.5), step_value)
    update = moment / correct / (jnp.sqrt(second / correct) + adam_eps) + decay_rate * weight
    fresh = weight - learn_rate * update
    return (fresh, fresh.astype(bf16), moment, second)


def ag(part):
    return lax.all_gather(part, "fsdp", axis=0, tiled=True)


def make_local(n_dp, n_f):

    def local(
        pixels,
        targets,
        valid_mask,
        lat_weight,
        segment_ids,
        present_vars,
        lead_index,
        step_count,
        w_agg,
        w_attn,
        w_mlp,
        w_io,
        w_small,
        m_agg,
        m_attn,
        m_mlp,
        m_io,
        m_small,
        v_agg,
        v_attn,
        v_mlp,
        v_io,
        v_small,
    ):
        masters = (w_agg, w_attn, w_mlp, w_io, w_small)
        firsts = (m_agg, m_attn, m_mlp, m_io, m_small)
        seconds = (v_agg, v_attn, v_mlp, v_io, v_small)
        rows = pixels.shape[1]
        row_len = segment_ids.shape[1]
        strip = w_agg.shape[0]
        own = lax.axis_index("fsdp")
        heads_here = HEADS // n_f
        wide = heads_here * HEAD_DIM
        seg = segment_ids[0]
        seg_own = lax.dynamic_slice_in_dim(seg, own * rows, rows)
        below = jnp.sum((seg[None, :] < seg_own[:, None]).astype(jnp.int32), axis=1)
        pos = own * rows + jnp.arange(rows, dtype=jnp.int32) - below
        onehot = (pos[:, None] == jnp.arange(SPAN, dtype=jnp.int32)[None, :]).astype(bf16)
        lead = (lead_index[0].astype(f32) + 1.0) / LEAD_STEPS
        pixel_rows = pixels[0]
        target = targets[0].astype(f32)
        present = present_vars[0]
        spread = (jnp.arange(MIX) // PIX)[None, :] == jnp.arange(VARS)[:, None]
        embed_col = (jnp.arange(MIX) - WIDTH)[None, :] == jnp.arange(VARS)[:, None]
        in_pixels = (jnp.arange(MIX) < WIDTH)[None, :]
        expand = jnp.where(in_pixels, spread, embed_col).astype(bf16)
        present_cols = jnp.repeat(present.astype(f32), PIX)
        pixel_weight = lat_weight[0][:, None] * valid_mask[0].astype(f32) * present_cols[None, :]
        total = lax.psum(jnp.sum(pixel_weight), ("dp", "fsdp"))
        pack = jnp.concatenate(
            [
                w_io[:, :USED].astype(bf16),
                w_small.astype(bf16),
                jnp.zeros((strip, 768 - USED - 9), bf16),
                w_agg.astype(bf16),
            ],
            axis=1,
        )
        head = lax.all_gather(pack, ("dp", "fsdp"), axis=0, tiled=True)
        attn = lax.all_gather(w_attn.astype(bf16), ("dp", "fsdp"), axis=0, tiled=True)
        mlp = lax.all_gather(w_mlp.astype(bf16), ("dp", "fsdp"), axis=0, tiled=True)
        w240 = jnp.concatenate([head[:, :WIDTH], head[:, 2 * WIDTH : 2 * WIDTH + VARS]], axis=1)
        w_pred = head[:, WIDTH : 2 * WIDTH]
        w_pos = head[:, 2 * WIDTH + VARS : USED]
        small = head[:, USED : USED + 9].astype(f32).T
        agg_kv = head[:, 768 : 768 + 2 * D]
        agg_out = head[:, 768 + 2 * D :]
        w_qkv = attn[:, : 3 * D]
        w_out = attn[:, 3 * D :]
        w_up = mlp[:, :FF]
        w_down = mlp[:, FF:]
        pix_t = jnp.concatenate([pixel_rows.T, jnp.ones((VARS, rows), bf16)], axis=0)
        table = t_mm(w240, agg_kv)
        table_k = table[:, :D].reshape(MIX, HEADS, HEAD_DIM)
        table_v = table[:, D:].reshape(MIX, HEADS, HEAD_DIM)
        query = small[0].reshape(HEADS, HEAD_DIM)
        folded = jnp.sum(table_k * query[None], axis=2)
        block = folded.T[:, None, :] * expand.astype(f32)[None]
        score = exact("xc,cl->xl", block.reshape(HEADS * VARS, MIX), pix_t.astype(f32))
        score = score.reshape(HEADS, VARS, rows) * HEAD_DIM ** (-0.5)
        score = jnp.where(present[None, :, None] > 0, score, -1000000000.0)
        top = jnp.max(score, axis=1, keepdims=True)
        power = jnp.exp(score - top)
        soft = power / jnp.sum(power, axis=1, keepdims=True)
        share = soft.astype(bf16)
        pix_f = pix_t.astype(f32)
        lifted_share = (
            jnp.einsum("vc,hvl->hcl", expand, share, preferred_element_type=f32) * pix_f[None]
        )
        mixed_a = exact("che,hcl->hel", table_v, lifted_share).reshape(D, rows).T.astype(bf16)
        lead_embed = lead * small[7] + small[8]
        h0 = mm(mixed_a, agg_out) + mm_t(onehot, w_pos) + lead_embed[None]
        norm0, unit0, scale0 = norm_forward(h0, small[1], small[2])
        qkv = mm(norm0, w_qkv).astype(bf16)
        part = qkv.reshape(rows, 3, n_f, wide)
        part = lax.all_to_all(part, "fsdp", split_axis=2, concat_axis=0, tiled=True)
        part = part.reshape(row_len, 3, heads_here, HEAD_DIM)
        q, k, v = (part[:, i].transpose(1, 0, 2) for i in range(3))
        att_score = jnp.einsum("hqe,hke->hqk", q, k, preferred_element_type=f32) * HEAD_DIM ** (
            -0.5
        )
        same = seg[:, None] == seg[None, :]
        att_score = jnp.where(same[None], att_score, -1000000000.0)
        att_top = jnp.max(att_score, axis=-1, keepdims=True)
        att_power = jnp.exp(att_score - att_top)
        att_soft = att_power / jnp.sum(att_power, axis=-1, keepdims=True)
        att = att_soft.astype(bf16)
        mixed_h = jnp.einsum("hqk,hke->qhe", att, v, preferred_element_type=f32)
        mixed_h = mixed_h.reshape(row_len, wide).astype(bf16)
        mixed_all = lax.all_gather(mixed_h, "fsdp", axis=1, tiled=True)
        mixed = lax.dynamic_slice_in_dim(mixed_all, own * rows, rows, axis=0)
        h1 = h0 + mm(mixed, w_out)
        norm1, unit1, scale1 = norm_forward(h1, small[3], small[4])
        up = mm(norm1, w_up)
        gate = 0.5 * (1.0 + lax.erf(up * 2.0 ** (-0.5)))
        lifted = (up * gate).astype(bf16)
        h2 = h1 + mm_t(lifted, w_down)
        norm2, unit2, scale2 = norm_forward(h2, small[5], small[6])
        predicted = mm(norm2, w_pred) * D ** (-0.5)
        error = predicted - target
        weighted = pixel_weight * error
        numerator = lax.psum(jnp.sum(weighted * error), ("dp", "fsdp"))
        d_pred = (weighted * (2.0 * D ** (-0.5) / total)).astype(bf16)
        d_norm2 = mm_t(d_pred, w_pred)
        d_h2, d_gain2, d_off2 = norm_backward(d_norm2, unit2, scale2, small[5])
        d_out = d_h2.astype(bf16)
        slope = gate + up * jnp.exp(-0.5 * up * up) * 0.3989422804014327
        d_up = (mm(d_out, w_down) * slope).astype(bf16)
        d_norm1 = mm_t(d_up, w_up)
        d_in, d_gain1, d_off1 = norm_backward(d_norm1, unit1, scale1, small[3])
        d_h1 = d_h2 + d_in
        d_proj_all = ag(d_h1.astype(bf16))
        w_out_own = lax.dynamic_slice_in_dim(w_out, own * wide, wide, axis=0)
        d_mixed = (
            mm_t(d_proj_all, w_out_own)
            .astype(bf16)
            .reshape(row_len, heads_here, HEAD_DIM)
            .transpose(1, 0, 2)
        )
        d_att = jnp.einsum("hqe,hke->hqk", d_mixed, v, preferred_element_type=f32)
        d_v = jnp.einsum("hqk,hqe->khe", att, d_mixed, preferred_element_type=f32)
        lean = jnp.sum(att_soft * d_att, axis=-1, keepdims=True)
        d_score = (att_soft * (d_att - lean) * HEAD_DIM ** (-0.5)).astype(bf16)
        d_q = jnp.einsum("hqk,hke->qhe", d_score, k, preferred_element_type=f32)
        d_k = jnp.einsum("hqk,hqe->khe", d_score, q, preferred_element_type=f32)
        d_part = jnp.stack([d_q, d_k, d_v], axis=1).astype(bf16).reshape(row_len, 3, 1, wide)
        d_qkv_all = lax.all_gather(d_part, "fsdp", axis=2, tiled=True).reshape(row_len, 3 * D)
        d_qkv = lax.dynamic_slice_in_dim(d_qkv_all, own * rows, rows, axis=0)
        d_norm0 = mm_t(d_qkv, w_qkv)
        d_in, d_gain0, d_off0 = norm_backward(d_norm0, unit0, scale0, small[1])
        d_h0 = d_h1 + d_in
        d_agg = d_h0.astype(bf16)
        d_mixed_a = mm_t(agg_out, d_agg).astype(bf16).reshape(HEADS, HEAD_DIM, rows)
        pulled = exact("che,hel->hcl", table_v, d_mixed_a.astype(f32)) * pix_f[None]
        d_share = exact("vc,hcl->hvl", expand.astype(f32), pulled)
        lean_a = jnp.sum(soft * d_share, axis=1, keepdims=True)
        d_score_a = (soft * (d_share - lean_a) * HEAD_DIM ** (-0.5)).astype(bf16)
        spread_score = jnp.einsum("vc,hvl->hcl", expand, d_score_a, preferred_element_type=f32)
        d_folded = jnp.sum(spread_score * pix_f[None], axis=2)
        d_table_v = exact("hcl,hel->che", lifted_share, d_mixed_a.astype(f32)).reshape(MIX, D)
        d_table_k = (d_folded.T[:, :, None] * query[None]).reshape(MIX, D)
        d_query = jnp.sum(d_folded.T[:, :, None] * table_k, axis=0).reshape(D)
        d_bias = jnp.sum(d_h0, axis=0)
        narrow = jnp.stack(
            [d_query, d_gain0, d_off0, d_gain1, d_off1, d_gain2, d_off2, lead * d_bias, d_bias]
            + [jnp.zeros((D,), f32)] * 7
        )
        d_table, narrow = lax.psum(
            (jnp.concatenate([d_table_k, d_table_v], axis=1), narrow), "fsdp"
        )

        def mine(array):
            whole = array.reshape(n_dp, n_f, strip, array.shape[1])
            return lax.dynamic_index_in_dim(whole, own, axis=1, keepdims=False).reshape(
                n_dp * strip, array.shape[1]
            )

        source = jnp.arange(D)
        pick = source // strip % n_f == own
        place = source // (strip * n_f) * strip + source % strip
        choose = (pick[:, None] & (place[:, None] == jnp.arange(n_dp * strip)[None, :])).astype(
            bf16
        )

        def weight_grad(features, grads):
            return t_mm(mm(features, choose).astype(bf16), grads)

        d_agg_all = ag(d_agg)
        g_attn = jnp.concatenate(
            [weight_grad(ag(norm0), d_qkv_all), weight_grad(mixed_all, d_proj_all)], axis=1
        )
        g_mlp = jnp.concatenate(
            [weight_grad(ag(norm1), ag(d_up)), weight_grad(ag(d_out), ag(lifted))], axis=1
        )
        g_out = weight_grad(ag(mixed_a), d_agg_all)
        g_kv = exact("dc,cx->dx", mine(w240).astype(f32), d_table)
        g_240 = exact("dx,cx->dc", mine(agg_kv).astype(f32), d_table)
        g_pred = weight_grad(ag(norm2), ag(d_pred))
        g_pos = weight_grad(d_agg_all, ag(onehot))
        g_small = mine(narrow.T)[:, :9]
        g_agg = jnp.concatenate([g_kv, g_out], axis=1)
        g_misc = jnp.concatenate(
            [
                g_240[:, :WIDTH],
                g_pred,
                g_240[:, WIDTH:],
                g_pos,
                g_small,
                jnp.zeros((n_dp * strip, 768 - USED - 9), f32),
            ],
            axis=1,
        )
        r_agg, r_attn, r_mlp, r_misc = (
            lax.psum_scatter(g, "dp", scatter_dimension=0, tiled=True)
            for g in (g_agg, g_attn, g_mlp, g_misc)
        )
        r_io = jnp.concatenate(
            [r_misc[:, :USED], jnp.zeros((strip, w_io.shape[1] - USED), f32)], axis=1
        )
        reduced = (r_agg, r_attn, r_mlp, r_io, r_misc[:, USED : USED + 9])
        squares = lax.psum(sum((jnp.sum(piece * piece) for piece in reduced)), ("dp", "fsdp"))
        grad_norm = jnp.sqrt(squares)
        factor = jnp.minimum(1.0, clip_limit / grad_norm)
        loss = numerator / total
        step_value = step_count[0].astype(f32)
        results = [
            adamw(
                masters[i], reduced[i] * factor, firsts[i], seconds[i], step_value, learn_rates[i]
            )
            for i in range(5)
        ]
        return (loss, grad_norm) + tuple((results[i][j] for j in range(4) for i in range(5)))

    return local


def solution(mesh):
    flat = P(("dp", "fsdp"), None)
    tokens = P("dp", "fsdp", None)
    return jax.shard_map(
        make_local(mesh.shape["dp"], mesh.shape["fsdp"]),
        mesh=mesh,
        in_specs=(
            tokens,
            tokens,
            tokens,
            P("dp", "fsdp"),
            P("dp", None),
            P("dp", None),
            P("dp"),
            P(),
        )
        + (flat,) * 15,
        out_specs=(P(), P()) + (flat,) * 20,
        check_vma=False,
    )
```

profile of v0, /device:TPU:0, one launch (start us, length us, event | category | flops | bytes accessed | tf_op | source)
XLA Modules:
  0.0 1196.0 jit_solution(15080212584497687655)
XLA Ops:
  16.4 73.1 %all-gather.15.cloned.1.call-done = bf16[1024,3840]{1,0:T(8,128)(2,1)} async-done(((bf16[32,3840]{1,0:T(8,128)(2,1)}), bf16[1024,3840]{1,0:T(8,128)(2,1)}) %all-gather.15.cloned.1.call-update) | async-done | bytes 7864336 | tf_op jit(solution)/shard_map/all_gather | solution.py:137
  112.8 56.2 %all-gather.17.cloned.1.call-done = bf16[1024,4096]{1,0:T(8,128)(2,1)} async-done(((bf16[32,4096]{1,0:T(8,128)(2,1)}), bf16[1024,4096]{1,0:T(8,128)(2,1)}) %all-gather.17.cloned.1.call-update) | async-done | bytes 8388624 | tf_op jit(solution)/shard_map/all_gather | solution.py:138
  184.0 10.5 all-to-all-done
  212.7 10.5 all-gather.19.cloned.1.call-done
  227.2 114.3 %all-gather.21.cloned.1.call-done = bf16[1024,8192]{1,0:T(8,128)(2,1)} async-done(((bf16[32,8192]{1,0:T(8,128)(2,1)}), bf16[1024,8192]{1,0:T(8,128)(2,1)}) %all-gather.21.cloned.1.call-update) | async-done | bytes 16777232 | tf_op jit(solution)/shard_map/all_gather | solution.py:139
  341.4 6.7 multiply_convert_fusion.1
  348.1 6.7 fusion.225
  359.7 39.0 %psum.36 = f32[]{:T(128)} all-reduce(f32[]{:T(128)} %get-tuple-element.166), channel_id=1, replica_groups=mesh['dp'=8,'fsdp'=4] {'dp','fsdp'}, use_global_device_ids=true, to_apply=%region_15.16 | all-reduce | flops 1 | bytes 8 | tf_op jit(solution)/shard_map/psum | solution.py:127
  405.1 7.0 fusion.19
  412.2 7.5 multiply_reduce_fusion.5
  424.0 14.7 %all-gather.23.cloned.1.call-done = bf16[512,1024]{1,0:T(8,128)(2,1)} async-done(((bf16[128,1024]{1,0:T(8,128)(2,1)}), bf16[512,1024]{1,0:T(8,128)(2,1)}) %all-gather.23.cloned.1.call-update) | async-done | bytes 1048592 | tf_op jit(solution)/shard_map/all_gather | solution.py:73
  447.8 8.1 fusion.73
  456.0 8.5 fusion.70
  467.5 27.7 %all-gather.25.cloned.1.call-done = bf16[512,3,4,256]{0,3,2,1:T(8,128)(2,1)} async-done(((bf16[512,3,1,256]{0,3,2,1:T(8,128)(2,1)}), bf16[512,3,4,256]{0,3,2,1:T(8,128)(2,1)}) %all-gather.25.cloned.1.call-update) | async-done | bytes 3145744 | tf_op jit(solution)/shard_map/all_gather | solution.py:225
  523.0 7.3 all_gather.63
  532.7 7.9 all_gather.62
  542.6 34.1 %all-reduce.6.cloned.1.call-done = (f32[240,2048]{0,1:T(8,128)}, f32[8,4,32,16]{2,1,0,3:T(4,128)}) async-done(((f32[240,2048]{0,1:T(8,128)}, f32[8,4,32,16]{2,1,0,3:T(4,128)}), (f32[240,2048]{0,1:T(8,128)}, f32[8,4,32,16]{2,1,0,3:T(4,128)})) %all-reduce.6.cloned.1.call-update) | async-done | bytes 2031632 | tf_op jit(solution)/shard_map/psum | solution.py:246
  581.4 14.3 %all-gather.29.cloned.1.call-done = bf16[512,1024]{1,0:T(8,128)(2,1)} async-done(((bf16[128,1024]{1,0:T(8,128)(2,1)}), bf16[512,1024]{1,0:T(8,128)(2,1)}) %all-gather.29.cloned.1.call-update) | async-done | bytes 1048592 | tf_op jit(solution)/shard_map/all_gather | solution.py:73
  603.0 10.9 all-gather.27.cloned.1.call-done
  623.0 10.0 all-gather.31.cloned.1.call-done
  641.0 10.7 all-gather.37.cloned.1.call-done
  651.7 36.7 %all-gather.39.cloned.1.call-done = bf16[512,4096]{1,0:T(8,128)(2,1)} async-done(((bf16[128,4096]{1,0:T(8,128)(2,1)}), bf16[512,4096]{1,0:T(8,128)(2,1)}) %all-gather.39.cloned.1.call-update) | async-done | bytes 4194320 | tf_op jit(solution)/shard_map/all_gather | solution.py:73
  688.3 6.7 fusion.86
  695.1 12.0 %all-gather.33.cloned.1.call-done = bf16[512,1024]{1,0:T(8,128)(2,1)} async-done(((bf16[128,1024]{1,0:T(8,128)(2,1)}), bf16[512,1024]{1,0:T(8,128)(2,1)}) %all-gather.33.cloned.1.call-update) | async-done | bytes 1048592 | tf_op jit(solution)/shard_map/all_gather | solution.py:73
  707.1 36.5 %all-gather.35.cloned.1.call-done = bf16[512,4096]{1,0:T(8,128)(2,1)} async-done(((bf16[128,4096]{1,0:T(8,128)(2,1)}), bf16[512,4096]{1,0:T(8,128)(2,1)}) %all-gather.35.cloned.1.call-update) | async-done | bytes 4194320 | tf_op jit(solution)/shard_map/all_gather | solution.py:73
  743.6 6.7 fusion.85
  750.3 7.6 pad_maximum_fusion
  758.7 50.6 %reduce-scatter.13.cloned.1.call-done = f32[32,768]{1,0:T(8,128)} async-done(((f32[256,768]{1,0:T(8,128)}), f32[32,768]{1,0:T(8,128)}) %reduce-scatter.13.cloned.1.call-update) | async-done | bytes 98320 | tf_op jit(solution)/shard_map/reduce_scatter | solution.py:292
  812.3 74.4 %reduce-scatter.7.cloned.1.call-done = f32[32,3072]{1,0:T(8,128)} async-done(((f32[256,3072]{1,0:T(8,128)}), f32[32,3072]{1,0:T(8,128)}) %reduce-scatter.7.cloned.1.call-update) | async-done | bytes 393232 | tf_op jit(solution)/shard_map/reduce_scatter | solution.py:292
  888.3 89.3 %reduce-scatter.9.cloned.1.call-done = f32[32,4096]{1,0:T(8,128)} async-done(((f32[256,4096]{1,0:T(8,128)}), f32[32,4096]{1,0:T(8,128)}) %reduce-scatter.9.cloned.1.call-update) | async-done | bytes 524304 | tf_op jit(solution)/shard_map/reduce_scatter | solution.py:292
  980.8 149.3 %reduce-scatter.11.cloned.1.call-done = f32[32,8192]{1,0:T(8,128)} async-done(((f32[256,8192]{1,0:T(8,128)}), f32[32,8192]{1,0:T(8,128)}) %reduce-scatter.11.cloned.1.call-update) | async-done | bytes 1048592 | tf_op jit(solution)/shard_map/reduce_scatter | solution.py:292
  1134.2 39.4 %all-reduce.2 = (f32[]{:T(128)}, f32[]{:T(128)}) all-reduce(f32[]{:T(128)} %get-tuple-element.167, f32[]{:T(128)S(6)} %add.312), channel_id=1, replica_groups=mesh['dp'=8,'fsdp'=4] {'dp','fsdp'}, use_global_device_ids=true, to_apply=%region_13.14 | all-reduce | flops 2 | bytes 16 | tf_op jit(solution)/shard_map/psum | solution.py:200
  (280 shorter events, 176.0 us)
Async XLA Ops:
  7.2 82.3 %all-gather.15.cloned.1.call-start = ((), (), s32[]{:S(2)}) async-start(), calls=%async_computation.5 | async-start | bytes 8110080 | tf_op jit(solution)/shard_map/all_gather | solution.py:137
  10.8 158.2 %all-gather.17.cloned.1.call-start = ((), (), s32[]{:S(2)}) async-start(), calls=%async_computation.6 | async-start | bytes 8650752 | tf_op jit(solution)/shard_map/all_gather | solution.py:138
  13.3 79.7 %copy-start.37 = (pred[240]{0:T(512)(128)(4,1)}, pred[240]{0:T(512)(128)(4,1)S(1)}, u32[]{:S(2)}) copy-start(pred[240]{0:T(512)(128)(4,1)S(1)} %iota_compare_fusion.5) | copy-start | bytes 724
  14.0 79.0 %copy-start.28 = (s32[240]{0:T(256)}, s32[240]{0:T(256)S(1)}, u32[]{:S(2)}) copy-start(s32[240]{0:T(256)S(1)} %get-tuple-element.225) | copy-start | bytes 2884
  14.0 79.0 %copy-start.30 = (s32[240]{0:T(256)}, s32[240]{0:T(256)S(1)}, u32[]{:S(2)}) copy-start(s32[240]{0:T(256)S(1)} %get-tuple-element.226) | copy-start | bytes 2884
  14.8 91.1 %copy-start.12 = (f32[240,128]{1,0:T(8,128)}, f32[240,128]{1,0:T(8,128)S(1)}, u32[]{:S(2)}) copy-start(f32[240,128]{1,0:T(8,128)S(1)} %pad_convert_fusion) | copy-start | bytes 368644
  15.7 86.7 %copy-start.47 = (s32[128]{0:T(128)}, s32[128]{0:T(128)S(1)}, u32[]{:S(2)}) copy-start(s32[128]{0:T(128)S(1)} %add_subtract_fusion) | copy-start | bytes 1540
  178.5 15.9 %all-to-all-start = ((bf16[128,3,4,256]{3,0,1,2:T(8,128)(2,1)}), bf16[128,3,4,256]{3,0,1,2:T(8,128)(2,1)}, u32[]{:S(2)}, u32[]{:S(2)}) async-start(bf16[128,3,4,256]{3,0,1,2:T(8,128)(2,1)} %copy.178), calls=%async_computation | async-start | bytes 1572864 | tf_op jit(solution)/shard_map/all_to_all | solution.py:174
  182.8 40.5 %all-gather.19.cloned.1.call-start = ((), (), s32[]{:S(2)}) async-start(), calls=%async_computation.7 | async-start | bytes 1310720 | tf_op jit(solution)/shard_map/all_gather | solution.py:188
  207.8 133.6 %all-gather.21.cloned.1.call-start = ((), (), s32[]{:S(2)}) async-start(), calls=%async_computation.8 | async-start | bytes 17301504 | tf_op jit(solution)/shard_map/all_gather | solution.py:139
  209.9 228.7 %all-gather.23.cloned.1.call-start = ((), (), s32[]{:S(2)}) async-start(), calls=%async_computation.9 | async-start | bytes 1310720 | tf_op jit(solution)/shard_map/all_gather | solution.py:73
  420.8 74.4 %all-gather.25.cloned.1.call-start = ((), (), s32[]{:S(2)}) async-start(), calls=%async_computation.10 | async-start | bytes 3932160 | tf_op jit(solution)/shard_map/all_gather | solution.py:225
  455.9 39.3 %copy-start.50 = (f32[128]{0:T(128)S(1)}, f32[128]{0:T(128)}, u32[]{:S(2)}) copy-start(f32[128]{0:T(128)} %copy-done.49) | copy-start | bytes 1540
  466.5 74.1 %all-gather.41.cloned.1.call-start = ((), (), s32[]{:S(2)}) async-start(), calls=%async_computation.21 | async-start | bytes 1310720 | tf_op jit(solution)/shard_map/all_gather | solution.py:73
  467.3 109.5 %all-reduce.6.cloned.1.call-start = ((), (), s32[]{:S(2)}) async-start(), calls=%async_computation.23 | async-start | bytes 4718592 | tf_op jit(solution)/shard_map/psum | solution.py:246
  518.3 77.4 %all-gather.29.cloned.1.call-start = ((), (), s32[]{:S(2)}) async-start(), calls=%async_computation.12 | async-start | bytes 1310720 | tf_op jit(solution)/shard_map/all_gather | solution.py:73
  519.0 94.9 %all-gather.27.cloned.1.call-start = ((), (), s32[]{:S(2)}) async-start(), calls=%async_computation.11 | async-start | bytes 1310720 | tf_op jit(solution)/shard_map/all_gather | solution.py:73
  519.6 113.3 %all-gather.31.cloned.1.call-start = ((), (), s32[]{:S(2)}) async-start(), calls=%async_computation.14 | async-start | bytes 1310720 | tf_op jit(solution)/shard_map/all_gather | solution.py:73
  520.4 131.3 %all-gather.37.cloned.1.call-start = ((), (), s32[]{:S(2)}) async-start(), calls=%async_computation.18 | async-start | bytes 1310720 | tf_op jit(solution)/shard_map/all_gather | solution.py:73
  520.9 167.4 %all-gather.39.cloned.1.call-start = ((), (), s32[]{:S(2)}) async-start(), calls=%async_computation.19 | async-start | bytes 5242880 | tf_op jit(solution)/shard_map/all_gather | solution.py:73
  521.7 185.4 %all-gather.33.cloned.1.call-start = ((), (), s32[]{:S(2)}) async-start(), calls=%async_computation.16 | async-start | bytes 1310720 | tf_op jit(solution)/shard_map/all_gather | solution.py:73
  522.3 221.3 %all-gather.35.cloned.1.call-start = ((), (), s32[]{:S(2)}) async-start(), calls=%async_computation.17 | async-start | bytes 5242880 | tf_op jit(solution)/shard_map/all_gather | solution.py:73
  522.9 286.4 %reduce-scatter.13.cloned.1.call-start = ((), (), s32[]{:S(2)}) async-start(), calls=%async_computation.22 | async-start | bytes 884736 | tf_op jit(solution)/shard_map/reduce_scatter | solution.py:292
  599.2 287.4 %reduce-scatter.7.cloned.1.call-start = ((), (), s32[]{:S(2)}) async-start(), calls=%async_computation.13 | async-start | bytes 3538944 | tf_op jit(solution)/shard_map/reduce_scatter | solution.py:292
  618.9 358.7 %reduce-scatter.9.cloned.1.call-start = ((), (), s32[]{:S(2)}) async-start(), calls=%async_computation.15 | async-start | bytes 4718592 | tf_op jit(solution)/shard_map/reduce_scatter | solution.py:292
  640.6 489.4 %reduce-scatter.11.cloned.1.call-start = ((), (), s32[]{:S(2)}) async-start(), calls=%async_computation.20 | async-start | bytes 9437184 | tf_op jit(solution)/shard_map/reduce_scatter | solution.py:292
  757.9 419.8 %copy-start.23 = (f32[32,9]{0,1:T(8,128)S(1)}, f32[32,9]{0,1:T(8,128)}, u32[]{:S(2)}) copy-start(f32[32,9]{0,1:T(8,128)} %param.35) | copy-start | bytes 3460
  757.9 421.2 %copy-start.14 = (f32[32,3072]{1,0:T(8,128)S(1)}, f32[32,3072]{1,0:T(8,128)}, u32[]{:S(2)}) copy-start(f32[32,3072]{1,0:T(8,128)} %param.31) | copy-start | bytes 1179652
  757.9 423.7 %copy-start.8 = (f32[32,4096]{1,0:T(8,128)S(1)}, f32[32,4096]{1,0:T(8,128)}, u32[]{:S(2)}) copy-start(f32[32,4096]{1,0:T(8,128)} %param.32) | copy-start | bytes 1572868
  977.6 204.0 %copy-start.9 = (f32[32,4096]{1,0:T(8,128)S(1)}, f32[32,4096]{1,0:T(8,128)}, u32[]{:S(2)}) copy-start(f32[32,4096]{1,0:T(8,128)} %reduce-scatter.9.cloned.1.call-done) | copy-start | bytes 1572868
  1132.1 52.2 %copy-start.4 = (f32[32,8192]{1,0:T(8,128)S(1)}, f32[32,8192]{1,0:T(8,128)}, u32[]{:S(2)}) copy-start(f32[32,8192]{1,0:T(8,128)} %param.33) | copy-start | bytes 3145732
  1132.1 52.2 %copy-start.5 = (f32[32,8192]{1,0:T(8,128)S(1)}, f32[32,8192]{1,0:T(8,128)}, u32[]{:S(2)}) copy-start(f32[32,8192]{1,0:T(8,128)} %reduce-scatter.11.cloned.1.call-done) | copy-start | bytes 3145732
  (45 other events, 277.1 us)
Sparse Core Ops, SparseCore 0:
  11.5 77.9 all-gather.14
  92.9 76.0 all-gather.16
  207.9 15.2 all-gather.18
  226.5 114.8 all-gather.20
  420.9 17.6 all-gather.22
  466.6 28.5 all-gather.24
  497.3 16.7 all-gather.40
  518.4 58.2 all-reduce.5
  578.9 16.7 all-gather.28
  597.1 16.8 all-gather.26
  616.1 16.7 all-gather.30
  634.9 16.7 all-gather.36
  653.8 34.4 all-gather.38
  690.3 16.7 all-gather.32
  709.1 34.4 all-gather.34
  746.7 62.4 reduce-scatter.12
  813.1 73.4 reduce-scatter.6
  890.6 87.0 reduce-scatter.8
  981.2 148.7 reduce-scatter.10
where the time goes:
time: 1200 us
  waiting for transfers between devices  841 us (70%)
  matrix products  137 us (11%)
  blocking collectives  93.6 us (8%)
  other arithmetic  58.3 us (5%)
  local copies, waits for them, and re-layouts  35.5 us (3%)
  between operations  25.1 us (2%)
    reduce_scatter x4, waiting for transfers between devices, local(): lax.psum_scatter(g, 'dp', scatter_dimension=0, tiled=True)  363 us
    all_gather x9, waiting for transfers between devices, ag(): return lax.all_gather(part, 'fsdp', axis=0, tiled=True)  146 us
    all_gather x1, waiting for transfers between devices, local(): mlp = lax.all_gather(w_mlp.astype(bf16), ('dp', 'fsdp'), axis=0, tiled=True)  114 us
    dot_general x21, matrix products, dot(): lax.dot_general(left, right, (dims, ((), ())), preferred_element_type=f32)  87.7 us
    all_gather x1, waiting for transfers between devices, local(): head = lax.all_gather(pack, ('dp', 'fsdp'), axis=0, tiled=True)  73.1 us
    all_gather x1, waiting for transfers between devices, local(): lax.all_gather(w_attn.astype(bf16), ('dp', 'fsdp'), axis=0, tiled=True)  56.2 us
    psum x1, blocking collectives, local(): numerator = lax.psum(jnp.sum(weighted * error), ('dp', 'fsdp'))  39.4 us
    psum x1, blocking collectives, local(): total = lax.psum(jnp.sum(pixel_weight), ('dp', 'fsdp'))  39 us
  transfers between devices with their start and end apart: 20, of which 19 were waited for; matrix products, arithmetic and copies ran while one was open for 10% of the time, Pallas kernels for 0%

commit v1 on v0

--- a/solution.py
+++ b/solution.py
@@ -70,7 +70,44 @@
 
 
 def ag(part):
-    return lax.all_gather(part, "fsdp", axis=0, tiled=True)
+
+    def write_the_signs(array_in):
+        block_last, row_out, current_value = (
+            lax.axis_size("fsdp"),
+            lax.axis_index("fsdp"),
+            array_in.shape[0],
+        )
+        r_now = lax.dynamic_update_slice_in_dim(
+            jnp.zeros(
+                [m * block_last if ii == 0 else m for ii, m in enumerate(array_in.shape)],
+                array_in.dtype,
+            ),
+            array_in,
+            row_out * current_value,
+            axis=0,
+        )
+        placed = low = array_in
+        for num in range(1, block_last // 2 + 1):
+            placed = lax.ppermute(
+                placed,
+                "fsdp",
+                perm=list(map(lambda ii: (ii, (ii + 1) % block_last), range(block_last))),
+            )
+            r_now = lax.dynamic_update_slice_in_dim(
+                r_now, placed, (row_out - num) % block_last * current_value, axis=0
+            )
+            if 2 * num < block_last:
+                low = lax.ppermute(
+                    low,
+                    "fsdp",
+                    list(map(lambda ii: (ii, (ii - 1) % block_last), range(block_last))),
+                )
+                r_now = lax.dynamic_update_slice_in_dim(
+                    r_now, low, (row_out + num) % block_last * current_value, axis=0
+                )
+        return r_now
+
+    return write_the_signs(part)
 
 
 def make_local(n_dp, n_f):

time: 1200 us -> 1060 us (0.88)
  waiting for transfers between devices: 841 us -> 646 us
  local copies, waits for them, and re-layouts: 35.5 us -> 80.5 us
  starting transfers between devices: 5.61 us -> 34.3 us
  blocking collectives: 93.6 us -> 78.3 us
    all_gather x9 -> x0, waiting for transfers between devices: 146 us -> none  [ag(): return lax.all_gather(part, 'fsdp', axis=0, tiled=True)]
    reduce_scatter x4, waiting for transfers between devices: 363 us -> 232 us  [local(): lax.psum_scatter(g, 'dp', scatter_dimension=0, tiled=True)]
    ppermute x0 -> x33, waiting for transfers between devices: none -> 108 us  [the longest x22 87.6 us: write_the_signs(): lax.ppermute(placed, 'fsdp', perm=list(map(lambda ii: (ii, (ii + 1) % blo...]
    ppermute x0 -> x33, starting transfers between devices: none -> 29.5 us  [the longest x22 21 us: write_the_signs(): lax.ppermute(placed, 'fsdp', perm=list(map(lambda ii: (ii, (ii + 1) % blo...]
    dynamic_update_slice x0 -> x35, local copies, waits for them, and re-layouts: none -> 29.3 us  [the longest x22 18.7 us: write_the_signs(): lax.dynamic_update_slice_in_dim(r_now, placed, (row_out - num) % block_la...]
    all_gather x1, waiting for transfers between devices: 27.7 us -> 0.02 us  [local(): lax.all_gather(d_part, 'fsdp', axis=2, tiled=True).reshape(row_len, 3 * D)]
    all_gather x2 -> x0, blocking collectives: 15.3 us -> none  [ag(): return lax.all_gather(part, 'fsdp', axis=0, tiled=True)]
  transfers between devices with their start and end apart: 20 -> 44, of which waited for: 19 -> 25; matrix products, arithmetic and copies ran while one was open for 10% -> 14% of each run, Pallas kernels for 0% -> 0%
where the time goes in v1:
time: 1060 us; the launch traced here: 1050 us
  waiting for transfers between devices  646 us (61%)
  matrix products  133 us (13%)
  local copies, waits for them, and re-layouts  80.5 us (8%)
  blocking collectives  78.3 us (7%)
  other arithmetic  56.2 us (5%)
  starting transfers between devices  34.3 us (3%)
  between operations  25.7 us (2%)
    reduce_scatter x4, waiting for transfers between devices, local(): lax.psum_scatter(g, 'dp', scatter_dimension=0, tiled=True)  232 us
    all_gather x1, waiting for transfers between devices, local(): mlp = lax.all_gather(w_mlp.astype(bf16), ('dp', 'fsdp'), axis=0, tiled=True)  114 us
    ppermute x22, waiting for transfers between devices, write_the_signs(): lax.ppermute(placed, 'fsdp', perm=list(map(lambda ii: (ii, (ii + 1) % blo...  87.6 us
    dot_general x21, matrix products, dot(): lax.dot_general(left, right, (dims, ((), ())), preferred_element_type=f32)  84 us
    all_gather x1, waiting for transfers between devices, local(): head = lax.all_gather(pack, ('dp', 'fsdp'), axis=0, tiled=True)  73.1 us
    all_gather x1, waiting for transfers between devices, local(): lax.all_gather(w_attn.astype(bf16), ('dp', 'fsdp'), axis=0, tiled=True)  56.5 us
    psum x1, waiting for transfers between devices, local(): lax.psum((jnp.concatenate([d_table_k, d_table_v], axis=1), narrow), 'fsdp')  42.1 us
    psum x1, blocking collectives, local(): numerator = lax.psum(jnp.sum(weighted * error), ('dp', 'fsdp'))  39.3 us
  transfers between devices with their start and end apart: 44, of which 25 were waited for; matrix products, arithmetic and copies ran while one was open for 14% of the time, Pallas kernels for 0%

profile of v1, /device:TPU:0, one launch (start us, length us, event | category | flops | bytes accessed | tf_op | source)
XLA Modules:
  0.0 1054.2 jit_solution(1515166546633543917)
XLA Ops:
  16.4 73.1 %all-gather.6.cloned.1.call-done = bf16[1024,3840]{1,0:T(8,128)(2,1)} async-done(((bf16[32,3840]{1,0:T(8,128)(2,1)}), bf16[1024,3840]{1,0:T(8,128)(2,1)}) %all-gather.6.cloned.1.call-update) | async-done | bytes 7864336 | tf_op jit(solution)/shard_map/all_gather | solution.py:174
  112.5 56.5 %all-gather.8.cloned.1.call-done = bf16[1024,4096]{1,0:T(8,128)(2,1)} async-done(((bf16[32,4096]{1,0:T(8,128)(2,1)}), bf16[1024,4096]{1,0:T(8,128)(2,1)}) %all-gather.8.cloned.1.call-update) | async-done | bytes 8388624 | tf_op jit(solution)/shard_map/all_gather | solution.py:175
  169.0 4.8 fusion.23
  183.9 10.5 all-to-all-done
  199.0 5.4 fusion.222
  212.8 10.5 all-gather.10.cloned.1.call-done
  227.9 113.6 %all-gather.12.cloned.1.call-done = bf16[1024,8192]{1,0:T(8,128)(2,1)} async-done(((bf16[32,8192]{1,0:T(8,128)(2,1)}), bf16[1024,8192]{1,0:T(8,128)(2,1)}) %all-gather.12.cloned.1.call-update) | async-done | bytes 16777232 | tf_op jit(solution)/shard_map/all_gather | solution.py:176
  344.0 6.8 constant_dynamic-update-slice_fusion.14
  350.8 6.8 fusion.224
  362.9 39.0 %psum.36 = f32[]{:T(128)} all-reduce(f32[]{:T(128)} %get-tuple-element.166), channel_id=1, replica_groups=mesh['dp'=8,'fsdp'=4] {'dp','fsdp'}, use_global_device_ids=true, to_apply=%region_15.16 | all-reduce | flops 1 | bytes 8 | tf_op jit(solution)/shard_map/psum | solution.py:164
  413.1 6.5 constant_dynamic-update-slice_fusion.22
  419.6 7.4 multiply_reduce_fusion.5
  431.0 4.6 collective-permute-done
  448.0 8.7 fusion.70
  456.7 8.4 fusion.73
  488.9 8.2 collective-permute-done.27
  503.6 6.4 collective-permute-done.29
  512.4 6.0 multiply_reduce_fusion.6
  545.2 8.2 collective-permute-done.7
  557.4 42.1 %all-reduce.6.cloned.1.call-done = (f32[240,2048]{0,1:T(8,128)}, f32[8,4,32,16]{2,1,0,3:T(4,128)}) async-done(((f32[240,2048]{0,1:T(8,128)}, f32[8,4,32,16]{2,1,0,3:T(4,128)}), (f32[240,2048]{0,1:T(8,128)}, f32[8,4,32,16]{2,1,0,3:T(4,128)})) %all-reduce.6.cloned.1.call-update) | async-done | bytes 2031632 | tf_op jit(solution)/shard_map/psum | solution.py:283
  620.9 6.2 collective-permute-done.9
  628.6 4.3 collective-permute-done.11
  646.6 17.5 %collective-permute-done.12 = bf16[128,1024]{1,0:T(8,128)(2,1)S(1)} collective-permute-done((bf16[128,1024]{1,0:T(8,128)(2,1)S(1)}, bf16[128,1024]{1,0:T(8,128)(2,1)S(1)}, u32[]{:S(2)}, u32[]{:S(2)}) %collective-permute-start.12) | collective-permute-done | bytes 262176 | tf_op jit(solution)/shard_map/ppermute | solution.py:91
  667.3 5.3 collective-permute-done.14
  676.3 24.4 %collective-permute-done.20 = bf16[128,1024]{1,0:T(8,128)(2,1)S(1)} collective-permute-done((bf16[128,1024]{1,0:T(8,128)(2,1)S(1)}, bf16[128,1024]{1,0:T(8,128)(2,1)S(1)}, u32[]{:S(2)}, u32[]{:S(2)}) %collective-permute-start.20) | collective-permute-done | bytes 262176 | tf_op jit(solution)/shard_map/ppermute | solution.py:91
  704.9 10.7 %collective-permute-done.22 = bf16[128,4096]{1,0:T(8,128)(2,1)S(1)} collective-permute-done((bf16[128,4096]{1,0:T(8,128)(2,1)S(1)}, bf16[128,4096]{1,0:T(8,128)(2,1)S(1)}, u32[]{:S(2)}, u32[]{:S(2)}) %collective-permute-start.22) | collective-permute-done | bytes 1048608 | tf_op jit(solution)/shard_map/ppermute | solution.py:100
  721.5 6.7 fusion.85
  732.7 6.8 fusion.86
  739.5 7.8 pad_maximum_fusion
  754.4 82.6 %reduce-scatter.9.cloned.1.call-done = f32[32,4096]{1,0:T(8,128)} async-done(((f32[256,4096]{1,0:T(8,128)}), f32[32,4096]{1,0:T(8,128)}) %reduce-scatter.9.cloned.1.call-update) | async-done | bytes 524304 | tf_op jit(solution)/shard_map/reduce_scatter | solution.py:329
  840.1 149.2 %reduce-scatter.11.cloned.1.call-done = f32[32,8192]{1,0:T(8,128)} async-done(((f32[256,8192]{1,0:T(8,128)}), f32[32,8192]{1,0:T(8,128)}) %reduce-scatter.11.cloned.1.call-update) | async-done | bytes 1048592 | tf_op jit(solution)/shard_map/reduce_scatter | solution.py:329
  993.3 39.3 %all-reduce.2 = (f32[]{:T(128)}, f32[]{:T(128)}) all-reduce(f32[]{:T(128)} %get-tuple-element.167, f32[]{:T(128)S(6)} %add.424), channel_id=1, replica_groups=mesh['dp'=8,'fsdp'=4] {'dp','fsdp'}, use_global_device_ids=true, to_apply=%region_13.14 | all-reduce | flops 2 | bytes 16 | tf_op jit(solution)/shard_map/psum | solution.py:237
  (444 shorter events, 234.2 us)
Async XLA Ops:
  7.2 82.3 %all-gather.6.cloned.1.call-start = ((), (), s32[]{:S(2)}) async-start(), calls=%async_computation.5 | async-start | bytes 8110080 | tf_op jit(solution)/shard_map/all_gather | solution.py:174
  10.8 158.2 %all-gather.8.cloned.1.call-start = ((), (), s32[]{:S(2)}) async-start(), calls=%async_computation.6 | async-start | bytes 8650752 | tf_op jit(solution)/shard_map/all_gather | solution.py:175
  178.5 15.9 %all-to-all-start = ((bf16[128,3,4,256]{3,0,1,2:T(8,128)(2,1)}), bf16[128,3,4,256]{3,0,1,2:T(8,128)(2,1)}, u32[]{:S(2)}, u32[]{:S(2)}) async-start(bf16[128,3,4,256]{3,0,1,2:T(8,128)(2,1)} %copy.206), calls=%async_computation | async-start | bytes 1572864 | tf_op jit(solution)/shard_map/all_to_all | solution.py:211
  182.7 40.6 %all-gather.10.cloned.1.call-start = ((), (), s32[]{:S(2)}) async-start(), calls=%async_computation.7 | async-start | bytes 1310720 | tf_op jit(solution)/shard_map/all_gather | solution.py:225
  207.9 133.6 %all-gather.12.cloned.1.call-start = ((), (), s32[]{:S(2)}) async-start(), calls=%async_computation.8 | async-start | bytes 17301504 | tf_op jit(solution)/shard_map/all_gather | solution.py:176
  210.0 302.3 %all-gather.14.cloned.1.call-start = ((), (), s32[]{:S(2)}) async-start(), calls=%async_computation.9 | async-start | bytes 3932160 | tf_op jit(solution)/shard_map/all_gather | solution.py:262
  469.2 130.3 %all-reduce.6.cloned.1.call-start = ((), (), s32[]{:S(2)}) async-start(), calls=%async_computation.14 | async-start | bytes 4718592 | tf_op jit(solution)/shard_map/psum | solution.py:283
  482.0 124.0 %collective-permute-start.3 = (bf16[128,1024]{0,1:T(8,128)(2,1)}, bf16[128,1024]{0,1:T(8,128)(2,1)}, u32[]{:S(2)}, u32[]{:S(2)}) collective-permute-start(bf16[128,1024]{0,1:T(8,128)(2,1)} %bitcast.197), channel_id=1, source_target_pairs={{0,1},{1,2},{2,3},{3,0},{4,5},{5,6},{6,7},{7,4},{8,9},{9,10},{10,1... | collective-permute-start | bytes 786440 | tf_op jit(solution)/shard_map/ppermute | solution.py:91
  484.4 124.6 %collective-permute-start.4 = (bf16[128,1024]{0,1:T(8,128)(2,1)}, bf16[128,1024]{0,1:T(8,128)(2,1)}, u32[]{:S(2)}, u32[]{:S(2)}) collective-permute-start(bf16[128,1024]{0,1:T(8,128)(2,1)} %bitcast.198), channel_id=1, source_target_pairs={{0,3},{1,0},{2,1},{3,2},{4,7},{5,4},{6,5},{7,6},{8,11},{9,8},{10,9... | collective-permute-start | bytes 786440 | tf_op jit(solution)/shard_map/ppermute | solution.py:100
  484.4 12.7 %collective-permute-start.27 = (bf16[128,192]{0,1:T(8,128)(2,1)S(1)}, bf16[128,192]{0,1:T(8,128)(2,1)S(1)}, u32[]{:S(2)}, u32[]{:S(2)}) collective-permute-start(bf16[128,192]{0,1:T(8,128)(2,1)S(1)} %copy-done.50), channel_id=1, source_target_pairs={{0,1},{1,2},{2,3},{3,0},{4,5},{5,6},{6,7},{7,4},{8,9},{9,10},{10,1... | collective-permute-start | bytes 147464 | tf_op jit(solution)/shard_map/ppermute | solution.py:91
  487.1 11.5 %collective-permute-start.28 = (bf16[128,192]{0,1:T(8,128)(2,1)S(1)}, bf16[128,192]{0,1:T(8,128)(2,1)S(1)}, u32[]{:S(2)}, u32[]{:S(2)}) collective-permute-start(bf16[128,192]{0,1:T(8,128)(2,1)S(1)} %copy-done.50), channel_id=1, source_target_pairs={{0,3},{1,0},{2,1},{3,2},{4,7},{5,4},{6,5},{7,6},{8,11},{9,8},{10,9... | collective-permute-start | bytes 147464 | tf_op jit(solution)/shard_map/ppermute | solution.py:100
  487.2 23.4 %collective-permute-start.24 = (bf16[128,1024]{1,0:T(8,128)(2,1)}, bf16[128,1024]{1,0:T(8,128)(2,1)}, u32[]{:S(2)}, u32[]{:S(2)}) collective-permute-start(bf16[128,1024]{1,0:T(8,128)(2,1)} %get-tuple-element.193), channel_id=1, source_target_pairs={{0,1},{1,2},{2,3},{3,0},{4,5},{5,6},{6,7},{7,4},{8,9},{9,10},{10,1... | collective-permute-start | bytes 786440 | tf_op jit(solution)/shard_map/ppermute | solution.py:91
  497.1 41.7 %collective-permute-start.25 = (bf16[128,1024]{1,0:T(8,128)(2,1)}, bf16[128,1024]{1,0:T(8,128)(2,1)}, u32[]{:S(2)}, u32[]{:S(2)}) collective-permute-start(bf16[128,1024]{1,0:T(8,128)(2,1)} %get-tuple-element.193), channel_id=1, source_target_pairs={{0,3},{1,0},{2,1},{3,2},{4,7},{5,4},{6,5},{7,6},{8,11},{9,8},{10,9... | collective-permute-start | bytes 786440 | tf_op jit(solution)/shard_map/ppermute | solution.py:100
  498.7 11.3 %collective-permute-start.29 = (bf16[128,192]{0,1:T(8,128)(2,1)S(1)}, bf16[128,192]{0,1:T(8,128)(2,1)S(1)}, u32[]{:S(2)}, u32[]{:S(2)}) collective-permute-start(bf16[128,192]{0,1:T(8,128)(2,1)S(1)} %collective-permute-done.27), channel_id=1, source_target_pairs={{0,1},{1,2},{2,3},{3,0},{4,5},{5,6},{6,7},{7,4},{8,9},{9,10},{10,1... | collective-permute-start | bytes 147464 | tf_op jit(solution)/shard_map/ppermute | solution.py:91
  510.6 29.9 %collective-permute-start.26 = (bf16[128,1024]{1,0:T(8,128)(2,1)}, bf16[128,1024]{1,0:T(8,128)(2,1)}, u32[]{:S(2)}, u32[]{:S(2)}) collective-permute-start(bf16[128,1024]{1,0:T(8,128)(2,1)} %collective-permute-done.24), channel_id=1, source_target_pairs={{0,1},{1,2},{2,3},{3,0},{4,5},{5,6},{6,7},{7,4},{8,9},{9,10},{10,1... | collective-permute-start | bytes 786440 | tf_op jit(solution)/shard_map/ppermute | solution.py:91
  527.6 14.6 %collective-permute-start.6 = (bf16[128,1024]{1,0:T(8,128)(2,1)}, bf16[128,1024]{1,0:T(8,128)(2,1)S(1)}, u32[]{:S(2)}, u32[]{:S(2)}) collective-permute-start(bf16[128,1024]{1,0:T(8,128)(2,1)} %get-tuple-element.208), channel_id=1, source_target_pairs={{0,1},{1,2},{2,3},{3,0},{4,5},{5,6},{6,7},{7,4},{8,9},{9,10},{10,1... | collective-permute-start | bytes 786440 | tf_op jit(solution)/shard_map/ppermute | solution.py:91
  538.7 209.4 %reduce-scatter.13.cloned.1.call-start = ((), (), s32[]{:S(2)}) async-start(), calls=%async_computation.13 | async-start | bytes 884736 | tf_op jit(solution)/shard_map/reduce_scatter | solution.py:329
  542.2 11.2 %collective-permute-start.7 = (bf16[128,1024]{1,0:T(8,128)(2,1)}, bf16[128,1024]{1,0:T(8,128)(2,1)S(1)}, u32[]{:S(2)}, u32[]{:S(2)}) collective-permute-start(bf16[128,1024]{1,0:T(8,128)(2,1)} %get-tuple-element.208), channel_id=1, source_target_pairs={{0,3},{1,0},{2,1},{3,2},{4,7},{5,4},{6,5},{7,6},{8,11},{9,8},{10,9... | collective-permute-start | bytes 786440 | tf_op jit(solution)/shard_map/ppermute | solution.py:100
  542.2 13.2 %collective-permute-start.8 = (bf16[128,1024]{1,0:T(8,128)(2,1)S(1)}, bf16[128,1024]{1,0:T(8,128)(2,1)S(1)}, u32[]{:S(2)}, u32[]{:S(2)}) collective-permute-start(bf16[128,1024]{1,0:T(8,128)(2,1)S(1)} %collective-permute-done.6), channel_id=1, source_target_pairs={{0,1},{1,2},{2,3},{3,0},{4,5},{5,6},{6,7},{7,4},{8,9},{9,10},{10,1... | collective-permute-start | bytes 786440 | tf_op jit(solution)/shard_map/ppermute | solution.py:91
  605.7 147.0 %reduce-scatter.7.cloned.1.call-start = ((), (), s32[]{:S(2)}) async-start(), calls=%async_computation.10 | async-start | bytes 3538944 | tf_op jit(solution)/shard_map/reduce_scatter | solution.py:329
  619.0 218.0 %reduce-scatter.9.cloned.1.call-start = ((), (), s32[]{:S(2)}) async-start(), calls=%async_computation.11 | async-start | bytes 4718592 | tf_op jit(solution)/shard_map/reduce_scatter | solution.py:329
  643.9 345.4 %reduce-scatter.11.cloned.1.call-start = ((), (), s32[]{:S(2)}) async-start(), calls=%async_computation.12 | async-start | bytes 9437184 | tf_op jit(solution)/shard_map/reduce_scatter | solution.py:329
  644.0 57.4 %collective-permute-start.15 = (bf16[128,4096]{1,0:T(8,128)(2,1)}, bf16[128,4096]{1,0:T(8,128)(2,1)S(1)}, u32[]{:S(2)}, u32[]{:S(2)}) collective-permute-start(bf16[128,4096]{1,0:T(8,128)(2,1)} %copy-done.88), channel_id=1, source_target_pairs={{0,1},{1,2},{2,3},{3,0},{4,5},{5,6},{6,7},{7,4},{8,9},{9,10},{10,1... | collective-permute-start | bytes 3145736 | tf_op jit(solution)/shard_map/ppermute | solution.py:91
  644.8 19.2 %collective-permute-start.12 = (bf16[128,1024]{1,0:T(8,128)(2,1)S(1)}, bf16[128,1024]{1,0:T(8,128)(2,1)S(1)}, u32[]{:S(2)}, u32[]{:S(2)}) collective-permute-start(bf16[128,1024]{1,0:T(8,128)(2,1)S(1)} %copy-done.38), channel_id=1, source_target_pairs={{0,1},{1,2},{2,3},{3,0},{4,5},{5,6},{6,7},{7,4},{8,9},{9,10},{10,1... | collective-permute-start | bytes 786440 | tf_op jit(solution)/shard_map/ppermute | solution.py:91
  644.9 21.7 %collective-permute-start.13 = (bf16[128,1024]{1,0:T(8,128)(2,1)S(1)}, bf16[128,1024]{1,0:T(8,128)(2,1)S(1)}, u32[]{:S(2)}, u32[]{:S(2)}) collective-permute-start(bf16[128,1024]{1,0:T(8,128)(2,1)S(1)} %copy-done.38), channel_id=1, source_target_pairs={{0,3},{1,0},{2,1},{3,2},{4,7},{5,4},{6,5},{7,6},{8,11},{9,8},{10,9... | collective-permute-start | bytes 786440 | tf_op jit(solution)/shard_map/ppermute | solution.py:100
  646.6 20.7 %collective-permute-start.18 = (bf16[128,1024]{1,0:T(8,128)(2,1)S(1)}, bf16[128,1024]{1,0:T(8,128)(2,1)S(1)}, u32[]{:S(2)}, u32[]{:S(2)}) collective-permute-start(bf16[128,1024]{1,0:T(8,128)(2,1)S(1)} %copy-done.43), channel_id=1, source_target_pairs={{0,1},{1,2},{2,3},{3,0},{4,5},{5,6},{6,7},{7,4},{8,9},{9,10},{10,1... | collective-permute-start | bytes 786440 | tf_op jit(solution)/shard_map/ppermute | solution.py:91
  666.6 36.2 %collective-permute-start.21 = (bf16[128,4096]{1,0:T(8,128)(2,1)S(1)}, bf16[128,4096]{1,0:T(8,128)(2,1)S(1)}, u32[]{:S(2)}, u32[]{:S(2)}) collective-permute-start(bf16[128,4096]{1,0:T(8,128)(2,1)S(1)} %copy-done.87), channel_id=1, source_target_pairs={{0,1},{1,2},{2,3},{3,0},{4,5},{5,6},{6,7},{7,4},{8,9},{9,10},{10,1... | collective-permute-start | bytes 3145736 | tf_op jit(solution)/shard_map/ppermute | solution.py:91
  667.3 33.4 %collective-permute-start.20 = (bf16[128,1024]{1,0:T(8,128)(2,1)S(1)}, bf16[128,1024]{1,0:T(8,128)(2,1)S(1)}, u32[]{:S(2)}, u32[]{:S(2)}) collective-permute-start(bf16[128,1024]{1,0:T(8,128)(2,1)S(1)} %collective-permute-done.18), channel_id=1, source_target_pairs={{0,1},{1,2},{2,3},{3,0},{4,5},{5,6},{6,7},{7,4},{8,9},{9,10},{10,1... | collective-permute-start | bytes 786440 | tf_op jit(solution)/shard_map/ppermute | solution.py:91
  673.3 30.5 %collective-permute-start.16 = (bf16[128,4096]{1,0:T(8,128)(2,1)}, bf16[128,4096]{1,0:T(8,128)(2,1)S(1)}, u32[]{:S(2)}, u32[]{:S(2)}) collective-permute-start(bf16[128,4096]{1,0:T(8,128)(2,1)} %copy-done.88), channel_id=1, source_target_pairs={{0,3},{1,0},{2,1},{3,2},{4,7},{5,4},{6,5},{7,6},{8,11},{9,8},{10,9... | collective-permute-start | bytes 3145736 | tf_op jit(solution)/shard_map/ppermute | solution.py:100
  674.0 41.6 %collective-permute-start.22 = (bf16[128,4096]{1,0:T(8,128)(2,1)S(1)}, bf16[128,4096]{1,0:T(8,128)(2,1)S(1)}, u32[]{:S(2)}, u32[]{:S(2)}) collective-permute-start(bf16[128,4096]{1,0:T(8,128)(2,1)S(1)} %copy-done.87), channel_id=1, source_target_pairs={{0,3},{1,0},{2,1},{3,2},{4,7},{5,4},{6,5},{7,6},{8,11},{9,8},{10,9... | collective-permute-start | bytes 3145736 | tf_op jit(solution)/shard_map/ppermute | solution.py:100
  701.4 19.0 %collective-permute-start.17 = (bf16[128,4096]{1,0:T(8,128)(2,1)S(1)}, bf16[128,4096]{1,0:T(8,128)(2,1)S(1)}, u32[]{:S(2)}, u32[]{:S(2)}) collective-permute-start(bf16[128,4096]{1,0:T(8,128)(2,1)S(1)} %collective-permute-done.15), channel_id=1, source_target_pairs={{0,1},{1,2},{2,3},{3,0},{4,5},{5,6},{6,7},{7,4},{8,9},{9,10},{10,1... | collective-permute-start | bytes 3145736 | tf_op jit(solution)/shard_map/ppermute | solution.py:91
  702.7 29.0 %collective-permute-start.23 = (bf16[128,4096]{1,0:T(8,128)(2,1)S(1)}, bf16[128,4096]{1,0:T(8,128)(2,1)S(1)}, u32[]{:S(2)}, u32[]{:S(2)}) collective-permute-start(bf16[128,4096]{1,0:T(8,128)(2,1)S(1)} %collective-permute-done.21), channel_id=1, source_target_pairs={{0,1},{1,2},{2,3},{3,0},{4,5},{5,6},{6,7},{7,4},{8,9},{9,10},{10,1... | collective-permute-start | bytes 3145736 | tf_op jit(solution)/shard_map/ppermute | solution.py:91
  (107 other events, 3159.0 us)
Sparse Core Ops, SparseCore 0:
  11.5 77.9 all-gather.5
  92.9 76.0 all-gather.7
  208.0 15.2 all-gather.9
  226.6 114.8 all-gather.11
  469.3 42.9 all-gather.13
  538.9 60.5 all-reduce.5
  605.8 62.5 reduce-scatter.12
  672.5 73.3 reduce-scatter.6
  750.0 87.0 reduce-scatter.8
  840.5 148.7 reduce-scatter.10
